TPU v7x, 32 devices: a whole 2x2x4 slice. The times are simulated.
32 devices in a mesh: prow: 8 (over y, x, core), pcol: 4 (over z).
Axes of the slice: x: 2, y: 2, z: 4, core: 2. Of those that a mesh axis runs over, the one named last changes fastest.
Arguments:
- matrix: float32 [4096, 4096], P('prow', 'pcol'), may hold values from -6 to 6
- pivots: int32 [2, 512], replicated, may hold values from 0 to 4095, as said below
- lower_inv: float32 [2, 512, 512], replicated, as said below
- upper_inv: float32 [2, 512, 512], replicated, as said below
Outputs:
- factored: float32 [4096, 4096], P('prow', 'pcol')
Inputs may be any that keep to these rules, and one draw needn't show every extreme that they name: The entries of pivots[k] are distinct row indices from k * 512 to 4095. Each lower_inv[k] is lower triangular. Each upper_inv[k] is upper triangular.
All inputs are finite; a program needn't handle non-finite values.
Results may differ from a plain program's by a relative error of at most 0.0001.
Values sent between devices are 32-bit elements; how exact they have to be, the bound alone decides.
No kernel may reach another device: no remote copies, remote signals or barrier semaphores. Data moves between devices by JAX's collectives and lax.ppermute only.
A program may use at most 128 MiB of HBM per device.

v0:
```python
import jax
import jax.numpy as jnp
from jax import lax
from jax.sharding import PartitionSpec as P


def broadcast(block, axis, holder):
    block = jnp.where(lax.axis_index(axis) == holder, block, jnp.zeros_like(block))
    return lax.psum(block, axis)


def displaced(pivot_row, start_row):
    width = pivot_row.shape[0]
    end_row = start_row + width
    window = start_row + jnp.arange(width, dtype=jnp.int32)
    chosen = jnp.any(pivot_row[None, :] == window[:, None], axis=1)
    unnamed = jnp.logical_not(chosen)
    free_rank = jnp.cumsum(unnamed.astype(jnp.int32)) - 1
    outside = pivot_row >= end_row
    out_rank = jnp.sum(
        (outside[None, :] & (pivot_row[None, :] < pivot_row[:, None])).astype(jnp.int32), axis=1
    )
    matches = unnamed[None, :] & (free_rank[None, :] == out_rank[:, None])
    source = jnp.sum(jnp.where(matches, window[None, :], 0), axis=1)
    return (source, outside)


def product(left, right):
    return jnp.dot(left, right, precision=lax.Precision.HIGHEST, preferred_element_type=jnp.float32)


def shards(matrix, pivots, lower_inv, upper_inv):
    local_rows, local_cols = matrix.shape
    block_width = lower_inv.shape[1]
    first_row = lax.axis_index("prow") * local_rows
    row_ids = first_row + jnp.arange(local_rows, dtype=jnp.int32)
    col_ids = lax.axis_index("pcol") * local_cols + jnp.arange(local_cols, dtype=jnp.int32)
    current = matrix
    for panel_index in range(pivots.shape[0]):
        start_row = panel_index * block_width
        end_row = start_row + block_width
        wanted = pivots[panel_index]
        offset = wanted - first_row
        owned_rows = (offset >= 0) & (offset < local_rows)
        gathered_rows = jnp.take(current, jnp.clip(offset, 0, local_rows - 1), axis=0)
        picked = jnp.where(owned_rows[:, None], gathered_rows, 0.0)
        beyond = col_ids >= end_row
        reduced = lax.psum_scatter(picked, "prow", scatter_dimension=0, tiled=True)
        raw_top = lax.all_gather(reduced, "prow", axis=0, tiled=True)
        solved = product(lower_inv[panel_index], raw_top)
        top_block = jnp.where(beyond[None, :], solved, raw_top)
        top_masked = jnp.where(beyond[None, :], solved, 0.0)
        owner_row = start_row // local_rows
        first_local = start_row - owner_row * local_rows
        local_top = current
        old_top = broadcast(local_top, "prow", owner_row)
        source, outside = displaced(wanted, start_row)
        dest_local = jnp.where(outside & owned_rows, offset, local_rows)
        moved = jnp.take(old_top, jnp.clip(source - start_row, 0, block_width - 1), axis=0)
        swapped = current.at[dest_local].set(moved, mode="drop")
        is_owner = lax.axis_index("prow") == owner_row
        top_slice = swapped
        swapped = swapped.at[first_local : first_local + block_width].set(
            jnp.where(is_owner, top_block, top_slice)
        )
        owner_col = start_row // local_cols
        left_col = start_row - owner_col * local_cols
        column_panel = product(
            swapped[:, left_col : left_col + block_width], upper_inv[panel_index]
        )
        lower_block = broadcast(column_panel, "pcol", owner_col)
        below_rows = row_ids >= end_row
        lower_masked = jnp.where(below_rows[:, None], lower_block, 0.0)
        updated = swapped - product(lower_masked, top_masked)
        panel_slice = updated[:, left_col : left_col + block_width]
        col_owner = lax.axis_index("pcol") == owner_col
        new_panel = jnp.where(below_rows[:, None] & col_owner, lower_block, panel_slice)
        current = updated.at[:, left_col : left_col + block_width].set(new_panel)
    return current


def solution(mesh):
    in_specs = (P("prow", "pcol"), P(), P(), P())
    out_specs = P("prow", "pcol")
    return jax.shard_map(shards, mesh=mesh, in_specs=in_specs, out_specs=out_specs, check_vma=False)
```

profile of v0, /device:TPU:0, one launch (start us, length us, event | category | flops | bytes accessed | tf_op | source)
XLA Modules:
  0.0 474.5 jit_solution(15905027569336554562)
XLA Ops:
  8.2 2.7 gather_fusion
  10.8 2.9 copy.50
  13.8 3.2 select_select_fusion.1
  17.0 2.9 copy.72
  21.8 3.1 broadcast_select_fusion.1
  25.0 39.0 %reduce-scatter.7.cloned.1.call-done = f32[64,1024]{1,0:T(8,128)} async-done(((f32[512,1024]{1,0:T(8,128)}), f32[64,1024]{1,0:T(8,128)}) %reduce-scatter.7.cloned.1.call-update) | async-done | bytes 262160 | tf_op jit(solution)/shard_map/reduce_scatter | solution.py:48
  65.9 63.2 %all-reduce.5.cloned.1.call-done = f32[512,1024]{0,1:T(8,128)} async-done(((f32[512,1024]{0,1:T(8,128)}), f32[512,1024]{0,1:T(8,128)}) %all-reduce.5.cloned.1.call-update) | async-done | bytes 2097168 | tf_op jit(solution)/shard_map/psum | solution.py:9
  129.0 2.9 copy.54
  131.9 19.5 %scatter_custom_fusion = f32[512,1024]{1,0:T(8,128)S(1)} fusion(f32[512,1024]{1,0:T(8,128)S(1)} %copy.85, s32[512]{0:T(512)S(1)} %bitcast.75, f32[]{:T(128)} %constant.160.clone.4, pred[512]{0:T(512)(128)(4,1)S(1)} %compare_and_fusion.2, f32[512,1024]{1,0:T(8,128)} %copy.54, s32[1024]{0:T(1024)S(1)} %pad_clamp_fusion.2), kind=kCustom, calls=%fused_computation.17 | custom fusion | flops 524288 | bytes 4198916 | tf_op jit(solution)/shard_map/scatter | solution.py:60
  153.2 5.0 %all-gather.3.cloned.1.call-done = f32[512,1024]{1,0:T(8,128)} async-done(((f32[64,1024]{1,0:T(8,128)}), f32[512,1024]{1,0:T(8,128)}) %all-gather.3.cloned.1.call-update) | async-done | bytes 2097168 | tf_op jit(solution)/shard_map/all_gather | solution.py:49
  158.2 2.9 copy.52
  161.1 10.8 %fusion.2 = (f32[512,1024]{0,1:T(8,128)S(1)}, f32[1024,512]{1,0:T(8,128)}) fusion(f32[512,1024]{0,1:T(8,128)} %copy.55, f32[512,1024]{0,1:T(8,128)} %copy.52, pred[1024]{0:T(1024)(128)(4,1)S(1)} %fusion.41, pred[]{:T(512)S(6)} %eq.31, f32[512,1024]{1,0:T(8,128)} %all-gather.3.cloned.1.call-done, f32[2,512,512]{2,1,0:T(8,128)} %param.20), kind=kOutput, calls=%fused_computation.12 | convolution fusion | flops 3222274048 | bytes 11535361 | tf_op jit(solution)/shard_map/dot_general | solution.py:29
  171.9 2.9 convolution_select_fusion.1
  175.7 51.7 %all-reduce.7.cloned.1.call-done = f32[512,512]{0,1:T(8,128)} async-done(((f32[512,512]{0,1:T(8,128)}), f32[512,512]{0,1:T(8,128)}) %all-reduce.7.cloned.1.call-update) | async-done | bytes 1048592 | tf_op jit(solution)/shard_map/psum | solution.py:9
  227.4 6.9 %fusion.8 = f32[512,1024]{0,1:T(8,128)} fusion(f32[512,1024]{0,1:T(8,128)S(1)} %get-tuple-element.86, f32[1024,512]{1,0:T(8,128)} %get-tuple-element.87, f32[512,512]{0,1:T(8,128)} %all-reduce.7.cloned.1.call-done, pred[1024]{0:T(1024)(128)(4,1)S(1)} %fusion.41, pred[512]{0:T(512)(128)(4,1)S(1)} %fusion.44), kind=kOutput, calls=%fused_computation.20 | convolution fusion | flops 3222536192 | bytes 7341568 | tf_op jit(solution)/shard_map/dot_general | solution.py:29
  234.3 3.0 fusion.10
  239.2 2.7 gather_fusion.1
  241.9 2.9 copy.59
  244.8 3.2 select_select_fusion
  248.0 2.9 copy.74
  252.6 39.1 %reduce-scatter.9.cloned.1.call-done = f32[64,1024]{1,0:T(8,128)} async-done(((f32[512,1024]{1,0:T(8,128)}), f32[64,1024]{1,0:T(8,128)}) %reduce-scatter.9.cloned.1.call-update) | async-done | bytes 262160 | tf_op jit(solution)/shard_map/reduce_scatter | solution.py:48
  293.0 63.5 %all-reduce.9.cloned.1.call-done = f32[512,1024]{0,1:T(8,128)} async-done(((f32[512,1024]{0,1:T(8,128)}), f32[512,1024]{0,1:T(8,128)}) %all-reduce.9.cloned.1.call-update) | async-done | bytes 2097168 | tf_op jit(solution)/shard_map/psum | solution.py:9
  356.5 2.9 copy.62
  359.4 19.6 %scatter_custom_fusion.1 = f32[512,1024]{1,0:T(8,128)S(1)} fusion(f32[512,1024]{1,0:T(8,128)S(1)} %copy.58, s32[512]{0:T(512)S(1)} %bitcast.74, f32[]{:T(128)} %constant.160.clone.4, pred[512]{0:T(512)(128)(4,1)S(1)} %compare_and_fusion, f32[512,1024]{1,0:T(8,128)} %copy.62, s32[1024]{0:T(1024)S(1)} %pad_clamp_fusion), kind=kCustom, calls=%fused_computation.14 | custom fusion | flops 524288 | bytes 4198916 | tf_op jit(solution)/shard_map/scatter | solution.py:60
  380.8 4.9 %all-gather.5.cloned.1.call-done = f32[512,1024]{1,0:T(8,128)} async-done(((f32[64,1024]{1,0:T(8,128)}), f32[512,1024]{1,0:T(8,128)}) %all-gather.5.cloned.1.call-update) | async-done | bytes 2097168 | tf_op jit(solution)/shard_map/all_gather | solution.py:49
  385.7 3.1 copy.61
  388.8 11.4 %fusion = (f32[512,1024]{0,1:T(8,128)S(1)}, f32[1024,512]{1,0:T(8,128)}) fusion(f32[512,1024]{0,1:T(8,128)} %copy.64, f32[512,1024]{0,1:T(8,128)} %copy.61, pred[1024]{0:T(1024)(128)(4,1)S(1)} %fusion.42, pred[]{:T(512)S(6)} %eq.30, f32[512,1024]{1,0:T(8,128)} %all-gather.5.cloned.1.call-done, f32[2,512,512]{2,1,0:T(8,128)} %param.20), kind=kOutput, calls=%fused_computation.8 | convolution fusion | flops 3222274048 | bytes 11535361 | tf_op jit(solution)/shard_map/dot_general | solution.py:29
  400.3 2.9 convolution_select_fusion
  403.2 51.9 %all-reduce.11.cloned.1.call-done = f32[512,512]{0,1:T(8,128)} async-done(((f32[512,512]{0,1:T(8,128)}), f32[512,512]{0,1:T(8,128)}) %all-reduce.11.cloned.1.call-update) | async-done | bytes 1048592 | tf_op jit(solution)/shard_map/psum | solution.py:9
  455.2 6.9 %fusion.9 = f32[512,1024]{0,1:T(8,128)} fusion(f32[512,1024]{0,1:T(8,128)S(1)} %get-tuple-element.88, f32[1024,512]{1,0:T(8,128)} %get-tuple-element.89, f32[512,512]{0,1:T(8,128)} %all-reduce.11.cloned.1.call-done, pred[1024]{0:T(1024)(128)(4,1)S(1)} %fusion.42, pred[512]{0:T(512)(128)(4,1)S(1)} %fusion.43), kind=kOutput, calls=%fused_computation.21 | convolution fusion | flops 3222536192 | bytes 7341568 | tf_op jit(solution)/shard_map/dot_general | solution.py:29
  462.1 2.5 fusion.11
  464.5 2.9 copy.67
  (70 shorter events, 14.9 us)
Async XLA Ops:
  6.5 1.6 copy-start.4
  6.5 57.4 %reduce-scatter.7.cloned.1.call-start = ((), (), s32[]{:S(2)}) async-start(), calls=%async_computation.8 | async-start | bytes 2359296 | tf_op jit(solution)/shard_map/reduce_scatter | solution.py:48
  19.9 109.1 %all-reduce.5.cloned.1.call-start = ((), (), s32[]{:S(2)}) async-start(), calls=%async_computation.3 | async-start | bytes 4194304 | tf_op jit(solution)/shard_map/psum | solution.py:9
  25.0 133.2 %all-gather.3.cloned.1.call-start = ((), (), s32[]{:S(2)}) async-start(), calls=%async_computation.2 | async-start | bytes 2359296 | tf_op jit(solution)/shard_map/all_gather | solution.py:49
  64.0 163.4 %all-reduce.7.cloned.1.call-start = ((), (), s32[]{:S(2)}) async-start(), calls=%async_computation.4 | async-start | bytes 2097152 | tf_op jit(solution)/shard_map/psum | solution.py:9
  161.1 10.8 %copy-start.2 = (f32[2,512,512]{2,1,0:T(8,128)S(1)}, f32[2,512,512]{2,1,0:T(8,128)}, u32[]{:S(2)}) copy-start(f32[2,512,512]{2,1,0:T(8,128)} %param.21) | copy-start | bytes 6291460
  174.8 116.8 %reduce-scatter.9.cloned.1.call-start = ((), (), s32[]{:S(2)}) async-start(), calls=%async_computation.9 | async-start | bytes 2359296 | tf_op jit(solution)/shard_map/reduce_scatter | solution.py:48
  227.4 6.9 %copy-start = (f32[512,512]{0,1:T(8,128)S(1)}, f32[512,512]{0,1:T(8,128)}, u32[]{:S(2)}) copy-start(f32[512,512]{0,1:T(8,128)} %all-reduce.7.cloned.1.call-done) | copy-start | bytes 3145732
  250.9 105.7 %all-reduce.9.cloned.1.call-start = ((), (), s32[]{:S(2)}) async-start(), calls=%async_computation.6 | async-start | bytes 4194304 | tf_op jit(solution)/shard_map/psum | solution.py:9
  252.5 133.2 %all-gather.5.cloned.1.call-start = ((), (), s32[]{:S(2)}) async-start(), calls=%async_computation.5 | async-start | bytes 2359296 | tf_op jit(solution)/shard_map/all_gather | solution.py:49
  291.7 163.5 %all-reduce.11.cloned.1.call-start = ((), (), s32[]{:S(2)}) async-start(), calls=%async_computation.7 | async-start | bytes 2097152 | tf_op jit(solution)/shard_map/psum | solution.py:9
  388.8 11.4 %copy-start.3 = (f32[2,512,512]{2,1,0:T(8,128)S(1)}, f32[2,512,512]{2,1,0:T(8,128)}, u32[]{:S(2)}) copy-start(f32[2,512,512]{2,1,0:T(8,128)} %param.21) | copy-start | bytes 6291460
  455.2 6.9 %copy-start.1 = (f32[512,512]{0,1:T(8,128)S(1)}, f32[512,512]{0,1:T(8,128)}, u32[]{:S(2)}) copy-start(f32[512,512]{0,1:T(8,128)} %all-reduce.11.cloned.1.call-done) | copy-start | bytes 3145732
Sparse Core Ops, SparseCore 0:
  20.0 43.8 reduce-scatter.6
  67.5 61.4 all-reduce.4
  131.1 27.0 all-gather.2
  175.0 52.4 all-reduce.6
  251.0 40.5 reduce-scatter.8
  295.1 61.4 all-reduce.8
  358.6 27.0 all-gather.4
  403.3 51.8 all-reduce.10
where the time goes:
time: 482 us; the launch traced here: 474 us
  waiting for transfers between devices  318 us (66%)
  other arithmetic  59 us (12%)
  matrix products  41.9 us (9%)
  local copies, waits for them, and re-layouts  41 us (9%)
  between operations  13.9 us (3%)
    psum x4, waiting for transfers between devices, broadcast(): return lax.psum(block, axis)  230 us
    reduce_scatter x2, waiting for transfers between devices, shards(): reduced = lax.psum_scatter(picked, 'prow', scatter_dimension=0, tiled=True)  78 us
    dot_general x6, matrix products, product(): jnp.dot(left, right, precision=lax.Precision.HIGHEST, preferred_element_t...  41.9 us
    scatter x2, other arithmetic, shards(): swapped = current.at[dest_local].set(moved, mode='drop')  39.1 us
    gather x4, local copies, waits for them, and re-layouts, shards(): jnp.take(current, jnp.clip(offset, 0, local_rows - 1), axis=0)  11.1 us
    all_gather x2, waiting for transfers between devices, shards(): raw_top = lax.all_gather(reduced, 'prow', axis=0, tiled=True)  9.83 us
  transfers between devices with their start and end apart: 8, of which 8 were waited for; matrix products, arithmetic and copies ran while one was open for 12% of the time, Pallas kernels for 0%

commit v1 on v0

--- a/solution.py
+++ b/solution.py
@@ -6,7 +6,7 @@
 
 def broadcast(block, axis, holder):
     block = jnp.where(lax.axis_index(axis) == holder, block, jnp.zeros_like(block))
-    return lax.psum(block, axis)
+    return jnp.sum(lax.all_gather(block, axis), axis=0)
 
 
 def displaced(pivot_row, start_row):

time: 482 us -> 713 us (1.48)
  waiting for transfers between devices: 318 us -> 473 us
  local copies, waits for them, and re-layouts: 41 us -> 91.4 us
  other arithmetic: 59 us -> 84.2 us
    all_gather x0 -> x4, waiting for transfers between devices: none -> 339 us  [broadcast(): return jnp.sum(lax.all_gather(block, axis), axis=0)]
    psum x4 -> x0, waiting for transfers between devices: 230 us -> none  [broadcast(): return lax.psum(block, axis)]
    all_gather x2, waiting for transfers between devices: 9.83 us -> 49.6 us  [shards(): raw_top = lax.all_gather(reduced, 'prow', axis=0, tiled=True)]
    unnamed x14 -> x12, local copies, waits for them, and re-layouts: 9.27 us -> 47.5 us
    reduce_sum x0 -> x4, other arithmetic: none -> 25.4 us  [broadcast(): return jnp.sum(lax.all_gather(block, axis), axis=0)]
    all_gather x0 -> x2, local copies, waits for them, and re-layouts: none -> 12.3 us  [broadcast(): return jnp.sum(lax.all_gather(block, axis), axis=0)]
  transfers between devices with their start and end apart: 8 -> 8, of which waited for: 8 -> 8; matrix products, arithmetic and copies ran while one was open for 12% -> 2% of each run, Pallas kernels for 0% -> 0%
where the time goes in v1:
time: 713 us; the launch traced here: 705 us
  waiting for transfers between devices  473 us (66%)
  local copies, waits for them, and re-layouts  91.4 us (13%)
  other arithmetic  84.2 us (12%)
  matrix products  41 us (6%)
  between operations  14.1 us (2%)
    all_gather x4, waiting for transfers between devices, broadcast(): return jnp.sum(lax.all_gather(block, axis), axis=0)  339 us
    reduce_scatter x2, waiting for transfers between devices, shards(): reduced = lax.psum_scatter(picked, 'prow', scatter_dimension=0, tiled=True)  83.9 us
    all_gather x2, waiting for transfers between devices, shards(): raw_top = lax.all_gather(reduced, 'prow', axis=0, tiled=True)  49.6 us
    unnamed x12, local copies, waits for them, and re-layouts  47.5 us
    dot_general x6, matrix products, product(): jnp.dot(left, right, precision=lax.Precision.HIGHEST, preferred_element_t...  41 us
    scatter x2, other arithmetic, shards(): swapped = current.at[dest_local].set(moved, mode='drop')  39 us
    reduce_sum x4, other arithmetic, broadcast(): return jnp.sum(lax.all_gather(block, axis), axis=0)  25.4 us
  transfers between devices with their start and end apart: 8, of which 8 were waited for; matrix products, arithmetic and copies ran while one was open for 2% of the time, Pallas kernels for 0%

profile of v1, /device:TPU:0, one launch (start us, length us, event | category | flops | bytes accessed | tf_op | source)
XLA Modules:
  0.0 704.5 jit_solution(2652224312785736082)
XLA Ops:
  10.8 2.9 copy.46
  13.8 3.2 select_select_fusion.1
  17.0 2.9 copy.68
  20.0 44.0 %reduce-scatter.7.cloned.1.call-done = f32[64,1024]{1,0:T(8,128)} async-done(((f32[512,1024]{1,0:T(8,128)}), f32[64,1024]{1,0:T(8,128)}) %reduce-scatter.7.cloned.1.call-update) | async-done | bytes 262160 | tf_op jit(solution)/shard_map/reduce_scatter | solution.py:48
  65.9 3.1 broadcast_select_fusion.1
  70.9 23.1 %all-gather.11.cloned.1.call-done = f32[512,1024]{1,0:T(8,128)} async-done(((f32[64,1024]{1,0:T(8,128)}), f32[512,1024]{1,0:T(8,128)}) %all-gather.11.cloned.1.call-update) | async-done | bytes 2097168 | tf_op jit(solution)/shard_map/all_gather | solution.py:49
  96.9 89.1 %all-gather.15.cloned.1.call-done = f32[4096,1024]{0,1:T(8,128)} async-done(((f32[512,1024]{0,1:T(8,128)}), f32[4096,1024]{0,1:T(8,128)}) %all-gather.15.cloned.1.call-update) | async-done | bytes 16777232 | tf_op jit(solution)/shard_map/all_gather | solution.py:9
  185.9 19.1 %copy.72 = f32[128,8,8,512]{3,2,1,0:T(8,128)S(1)} copy(f32[128,8,8,512]{3,1,2,0:T(8,128)} %bitcast.82) | data formatting | bytes 33554432
  205.1 8.0 %bitcast_reduce_fusion.1 = f32[512,1024]{0,1:T(8,128)} fusion(f32[128,8,8,512]{3,2,1,0:T(8,128)S(1)} %copy.72), kind=kLoop, calls=%fused_computation.7 | loop fusion | flops 3670016 | bytes 18874368 | tf_op jit(solution)/shard_map/reduce_sum | solution.py:9
  213.1 2.9 copy.50
  216.0 19.2 %scatter_custom_fusion = f32[512,1024]{1,0:T(8,128)S(1)} fusion(f32[512,1024]{1,0:T(8,128)S(1)} %copy.79, s32[512]{0:T(512)S(1)} %bitcast.91, f32[]{:T(128)} %constant.160.clone.4, pred[512]{0:T(512)(128)(4,1)S(1)} %compare_and_fusion.2, f32[512,1024]{1,0:T(8,128)} %copy.50, s32[1024]{0:T(1024)S(1)} %pad_clamp_fusion.2), kind=kCustom, calls=%fused_computation.19 | custom fusion | flops 524288 | bytes 4198916 | tf_op jit(solution)/shard_map/scatter | solution.py:60
  237.0 10.8 %fusion.2 = (f32[512,1024]{0,1:T(8,128)S(1)}, f32[1024,512]{1,0:T(8,128)}) fusion(f32[512,1024]{0,1:T(8,128)} %copy.51, f32[512,1024]{0,1:T(8,128)} %copy.48, pred[1024]{0:T(1024)(128)(4,1)S(1)} %fusion.41, pred[]{:T(512)S(6)} %eq.31, f32[512,1024]{1,0:T(8,128)} %all-gather.11.cloned.1.call-done, f32[2,512,512]{2,1,0:T(8,128)} %param.20), kind=kOutput, calls=%fused_computation.14 | convolution fusion | flops 3222274048 | bytes 11535361 | tf_op jit(solution)/shard_map/dot_general | solution.py:29
  247.8 2.9 convolution_select_fusion.1
  252.0 80.4 %all-gather.17.cloned.1.call-done = f32[2048,512]{0,1:T(8,128)} async-done(((f32[512,512]{0,1:T(8,128)}), f32[2048,512]{0,1:T(8,128)}) %all-gather.17.cloned.1.call-update) | async-done | bytes 4194320 | tf_op jit(solution)/shard_map/all_gather | solution.py:9
  332.3 6.0 reshape.355
  338.3 4.7 reduce_sum.75
  343.0 6.5 fusion.8
  349.5 3.0 fusion.10
  360.0 3.2 select_select_fusion
  366.1 39.9 %reduce-scatter.9.cloned.1.call-done = f32[64,1024]{1,0:T(8,128)} async-done(((f32[512,1024]{1,0:T(8,128)}), f32[64,1024]{1,0:T(8,128)}) %reduce-scatter.9.cloned.1.call-update) | async-done | bytes 262160 | tf_op jit(solution)/shard_map/reduce_scatter | solution.py:48
  409.2 26.5 %all-gather.13.cloned.1.call-done = f32[512,1024]{1,0:T(8,128)} async-done(((f32[64,1024]{1,0:T(8,128)}), f32[512,1024]{1,0:T(8,128)}) %all-gather.13.cloned.1.call-update) | async-done | bytes 2097168 | tf_op jit(solution)/shard_map/all_gather | solution.py:49
  438.6 88.9 %all-gather.19.cloned.1.call-done = f32[4096,1024]{0,1:T(8,128)} async-done(((f32[512,1024]{0,1:T(8,128)}), f32[4096,1024]{0,1:T(8,128)}) %all-gather.19.cloned.1.call-update) | async-done | bytes 16777232 | tf_op jit(solution)/shard_map/all_gather | solution.py:9
  527.5 19.1 %copy.73 = f32[128,8,8,512]{3,2,1,0:T(8,128)S(1)} copy(f32[128,8,8,512]{3,1,2,0:T(8,128)} %bitcast.83) | data formatting | bytes 33554432
  546.6 8.0 %bitcast_reduce_fusion = f32[512,1024]{0,1:T(8,128)} fusion(f32[128,8,8,512]{3,2,1,0:T(8,128)S(1)} %copy.73), kind=kLoop, calls=%fused_computation.6 | loop fusion | flops 3670016 | bytes 18874368 | tf_op jit(solution)/shard_map/reduce_sum | solution.py:9
  554.6 2.9 copy.58
  557.6 19.8 %scatter_custom_fusion.1 = f32[512,1024]{1,0:T(8,128)S(1)} fusion(f32[512,1024]{1,0:T(8,128)S(1)} %copy.54, s32[512]{0:T(512)S(1)} %bitcast.90, f32[]{:T(128)} %constant.160.clone.4, pred[512]{0:T(512)(128)(4,1)S(1)} %compare_and_fusion, f32[512,1024]{1,0:T(8,128)} %copy.58, s32[1024]{0:T(1024)S(1)} %pad_clamp_fusion), kind=kCustom, calls=%fused_computation.16 | custom fusion | flops 524288 | bytes 4198916 | tf_op jit(solution)/shard_map/scatter | solution.py:60
  579.2 11.4 %fusion = (f32[512,1024]{0,1:T(8,128)S(1)}, f32[1024,512]{1,0:T(8,128)}) fusion(f32[512,1024]{0,1:T(8,128)} %copy.60, f32[512,1024]{0,1:T(8,128)} %copy.57, pred[1024]{0:T(1024)(128)(4,1)S(1)} %fusion.42, pred[]{:T(512)S(6)} %eq.30, f32[512,1024]{1,0:T(8,128)} %all-gather.13.cloned.1.call-done, f32[2,512,512]{2,1,0:T(8,128)} %param.20), kind=kOutput, calls=%fused_computation.10 | convolution fusion | flops 3222274048 | bytes 11535361 | tf_op jit(solution)/shard_map/dot_general | solution.py:29
  590.6 2.9 convolution_select_fusion
  593.6 80.9 %all-gather.21.cloned.1.call-done = f32[2048,512]{0,1:T(8,128)} async-done(((f32[512,512]{0,1:T(8,128)}), f32[2048,512]{0,1:T(8,128)}) %all-gather.21.cloned.1.call-update) | async-done | bytes 4194320 | tf_op jit(solution)/shard_map/all_gather | solution.py:9
  674.5 6.2 reshape.357
  680.7 4.7 reduce_sum.79
  685.4 6.5 fusion.9
  (74 shorter events, 37.5 us)
Async XLA Ops:
  6.5 1.6 copy-start.2
  6.5 57.4 %reduce-scatter.7.cloned.1.call-start = ((), (), s32[]{:S(2)}) async-start(), calls=%async_computation.8 | async-start | bytes 2359296 | tf_op jit(solution)/shard_map/reduce_scatter | solution.py:48
  19.9 74.0 %all-gather.11.cloned.1.call-start = ((), (), s32[]{:S(2)}) async-start(), calls=%async_computation.2 | async-start | bytes 2359296 | tf_op jit(solution)/shard_map/all_gather | solution.py:49
  64.0 121.9 %all-gather.15.cloned.1.call-start = ((), (), s32[]{:S(2)}) async-start(), calls=%async_computation.4 | async-start | bytes 18874368 | tf_op jit(solution)/shard_map/all_gather | solution.py:9
  69.0 263.3 %all-gather.17.cloned.1.call-start = ((), (), s32[]{:S(2)}) async-start(), calls=%async_computation.5 | async-start | bytes 5242880 | tf_op jit(solution)/shard_map/all_gather | solution.py:9
  237.0 10.8 %copy-start = (f32[2,512,512]{2,1,0:T(8,128)S(1)}, f32[2,512,512]{2,1,0:T(8,128)}, u32[]{:S(2)}) copy-start(f32[2,512,512]{2,1,0:T(8,128)} %param.21) | copy-start | bytes 6291460
  250.8 155.2 %reduce-scatter.9.cloned.1.call-start = ((), (), s32[]{:S(2)}) async-start(), calls=%async_computation.9 | async-start | bytes 2359296 | tf_op jit(solution)/shard_map/reduce_scatter | solution.py:48
  366.1 69.6 %all-gather.13.cloned.1.call-start = ((), (), s32[]{:S(2)}) async-start(), calls=%async_computation.3 | async-start | bytes 2359296 | tf_op jit(solution)/shard_map/all_gather | solution.py:49
  406.0 121.5 %all-gather.19.cloned.1.call-start = ((), (), s32[]{:S(2)}) async-start(), calls=%async_computation.6 | async-start | bytes 18874368 | tf_op jit(solution)/shard_map/all_gather | solution.py:9
  407.7 266.8 %all-gather.21.cloned.1.call-start = ((), (), s32[]{:S(2)}) async-start(), calls=%async_computation.7 | async-start | bytes 5242880 | tf_op jit(solution)/shard_map/all_gather | solution.py:9
  579.2 11.4 %copy-start.1 = (f32[2,512,512]{2,1,0:T(8,128)S(1)}, f32[2,512,512]{2,1,0:T(8,128)}, u32[]{:S(2)}) copy-start(f32[2,512,512]{2,1,0:T(8,128)} %param.21) | copy-start | bytes 6291460
Sparse Core Ops, SparseCore 0:
  20.0 43.8 reduce-scatter.6
  66.0 27.8 all-gather.10
  96.0 89.8 all-gather.14
  250.9 81.3 all-gather.16
  366.2 39.7 reduce-scatter.8
  407.8 27.8 all-gather.12
  437.6 89.8 all-gather.18
  593.7 80.7 all-gather.20
